TPU v7x, 256 devices: a whole 4x4x8 slice. The times are simulated.
256 devices in a mesh: lat: 4 (over z_lo, core), lon: 16 (over z_hi, y), tm: 4 (over x).
Axes of the slice: x: 4, y: 4, z: 8 (z_hi: 4, z_lo: 2; z = z_hi * 2 + z_lo), core: 2. Of those that a mesh axis runs over, the one named last changes fastest.
Arguments:
- signal: bfloat16 [4, 78, 32, 2048], P('tm', None, 'lat', 'lon'), may hold values from -6 to 6
- dictionary: bfloat16 [64, 9984], P('lon'), may hold values from -0.0625 to 0.0625
- codes_init: float32 [4, 64, 8, 512], P('tm', None, 'lat', 'lon'), may hold values from -3 to 3
- thresholds: float32 [64], replicated, may hold values from 0.2 to 2
Outputs:
- codes: float32 [4, 64, 8, 512], P('tm', None, 'lat', 'lon')
- dict_grad: float32 [64, 9984], P('lon')
All inputs are finite; a program needn't handle non-finite values.
Results may differ from a plain program's by a relative error of at most 0.0044.
Values may be sent and summed in bfloat16 or wider, within the bound.
No kernel may reach another device: no remote copies, remote signals or barrier semaphores. Data moves between devices by JAX's collectives and lax.ppermute only.
A program may use at most 128 MiB of HBM per device.

v0:
```python
import math
import jax
import jax.numpy as jnp
from jax import lax
from jax.sharding import PartitionSpec as P

ITERS = 2
STEP_SIZE = 0.5


def passed_along(shard, axis, by):
    peers = lax.axis_size(axis)
    pairs = [(i, i + by) for i in range(peers) if 0 <= i + by < peers]
    return lax.ppermute(shard, axis, pairs)


def shifted(block, axis, distance):
    devices = range(lax.axis_size(axis))
    route = [((i - distance) % len(devices), i) for i in devices]
    return lax.ppermute(block, axis, route)


def combos():
    return [(delay, down, right) for delay in (0, 1) for down in (0, 1) for right in (0, 1)]


def to_atoms(local, channels, count):
    shaped = local.reshape(channels, 4, 4, 2, 2, 2, count)
    return shaped.transpose(6, 3, 0, 4, 1, 5, 2).reshape(count, 2 * channels * 64)


def extend_codes(coded):
    atoms, rows, columns = coded.shape
    earlier = passed_along(coded, "tm", 1)
    both = jnp.stack([coded, earlier])
    above = passed_along(both[:, :, -1:, :], "lat", 1)
    both = jnp.concatenate([above, both], axis=2)
    beside = shifted(both[:, :, :, -1:], "lon", 1)
    both = jnp.concatenate([beside, both], axis=3)
    pieces = [
        both[delay, :, 1 - down : 1 - down + rows, 1 - right : 1 - right + columns]
        for delay, down, right in combos()
    ]
    return jnp.stack(pieces).reshape(8 * atoms, rows * columns)


def body(signal, dictionary, codes_init, thresholds):
    channels = signal.shape[1]
    rows = signal.shape[2] // 4
    columns = signal.shape[3] // 4
    patch = channels * 16
    gathered = lax.all_gather(dictionary, "lon", axis=0, tiled=True)
    atoms = gathered.shape[0]
    blocks = (
        gathered.reshape(atoms, 2, channels, 2, 4, 2, 4)
        .transpose(1, 3, 5, 2, 4, 6, 0)
        .reshape(8, patch, atoms)
    )
    synth_matrix = blocks.transpose(1, 0, 2).reshape(patch, 8 * atoms)
    target = (
        signal[0]
        .reshape(channels, rows, 4, columns, 4)
        .transpose(0, 2, 4, 1, 3)
        .reshape(patch, rows * columns)
    )

    def residual_of(current):
        stacked = extend_codes(current.astype(jnp.bfloat16).reshape(atoms, rows, columns))
        synth = jnp.dot(synth_matrix, stacked, preferred_element_type=jnp.float32)
        return ((synth - target).astype(jnp.bfloat16), stacked)

    adjoint_matrix = blocks.transpose(2, 0, 1).reshape(atoms, 8 * patch)
    current = codes_init[0].reshape(atoms, rows * columns)
    moving = current
    momentum_now = 1.0
    shrink = STEP_SIZE * thresholds[:, None]
    for turn in range(ITERS):
        residual, stacked = residual_of(moving)
        frame = residual.reshape(patch, rows, columns)
        later = passed_along(frame, "tm", -1)
        both = jnp.stack([frame, later])
        below = passed_along(both[:, :, :1, :], "lat", -1)
        both = jnp.concatenate([both, below], axis=2)
        beside = shifted(both[:, :, :, :1], "lon", -1)
        both = jnp.concatenate([both, beside], axis=3)
        pieces = [
            both[delay, :, down : down + rows, right : right + columns]
            for delay, down, right in combos()
        ]
        adjoint_stacked = jnp.stack(pieces).reshape(8 * patch, rows * columns)
        descent = moving - STEP_SIZE * jnp.dot(
            adjoint_matrix, adjoint_stacked, preferred_element_type=jnp.float32
        )
        updated = jnp.sign(descent) * jnp.maximum(jnp.abs(descent) - shrink, 0.0)
        momentum_next = (1.0 + math.sqrt(1.0 + 4.0 * momentum_now * momentum_now)) / 2.0
        moving = updated + (momentum_now - 1.0) / momentum_next * (updated - current)
        current = updated
        momentum_now = momentum_next
    residual, stacked = residual_of(current)
    positions = lax.axis_size("tm") * lax.axis_size("lat") * lax.axis_size("lon") * rows * columns
    scale = 1.0 / math.sqrt(positions)
    owned_rows = atoms // lax.axis_size("lon")
    local = lax.dot_general(
        residual, stacked, (((1,), (1,)), ((), ())), preferred_element_type=jnp.float32
    )
    total = lax.psum(to_atoms(local, channels, atoms) * scale, ("lat", "lon", "tm"))
    mine = lax.dynamic_slice_in_dim(total, lax.axis_index("lon") * owned_rows, owned_rows, 0)
    return (current.reshape(1, atoms, rows, columns), mine)


def solution(mesh):
    placed = (P("tm", None, "lat", "lon"), P("lon", None), P("tm", None, "lat", "lon"), P())
    return jax.shard_map(
        body,
        mesh=mesh,
        in_specs=placed,
        out_specs=(P("tm", None, "lat", "lon"), P("lon", None)),
        check_vma=False,
    )
```

profile of v0, /device:TPU:2, one launch (start us, length us, event | category | flops | bytes accessed | tf_op | source)
XLA Modules:
  0.0 632.7 jit_solution(5299699721707933311)
XLA Ops:
  8.7 3.4 collective-permute-start
  12.1 2.2 collective-permute-done
  21.6 5.3 collective-permute-done.2
  27.2 40.2 %all-gather.3.cloned.1.call-done = bf16[16,4,9984]{2,1,0:T(4,128)(2,1)} async-done(((bf16[1,4,9984]{2,1,0:T(4,128)(2,1)}), bf16[16,4,9984]{2,1,0:T(4,128)(2,1)}) %all-gather.3.cloned.1.call-update) | async-done | bytes 1277968 | tf_op jit(solution)/shard_map/all_gather | solution.py:52
  67.5 89.3 %reshape.84 = bf16[64,2,78,2,4,2,4]{6,5,4,3,2,1,0:T(2,128)(2,1)} reshape(bf16[16,4,9984]{2,1,0:T(4,128)(2,1)} %all-gather.3.cloned.1.call-done) | data formatting | bytes 2555904 | tf_op jit(solution)/shard_map/reshape | solution.py:55
  156.8 86.1 %copy.69 = bf16[64,2,78,2,4,2,4]{0,6,4,2,5,3,1:T(4,128)(2,1)S(1)} copy(bf16[64,2,78,2,4,2,4]{6,5,4,3,2,1,0:T(2,128)(2,1)} %reshape.84) | data formatting | bytes 2555904 | tf_op jit(solution)/shard_map/transpose | solution.py:56
  242.8 2.8 copy.51
  247.3 2.5 collective-permute-start.3
  249.8 4.7 collective-permute-done.3
  255.9 2.0 collective-permute-done.4
  257.9 3.9 collective-permute-start.5
  265.5 3.5 reshape.68
  269.0 1.9 fusion.15
  270.9 3.4 collective-permute-start.6
  274.3 2.2 collective-permute-done.6
  276.5 2.2 collective-permute-start.7
  279.6 8.1 %collective-permute-done.8 = bf16[2,64,3,1]{1,3,2,0:T(2,128)(2,1)S(1)} collective-permute-done((bf16[2,64,3,1]{1,3,2,0:T(2,128)(2,1)S(1)}, bf16[2,64,3,1]{1,3,2,0:T(2,128)(2,1)S(1)}, u32[]{:S(2)}, u32[]{:S(2)}) %collective-permute-start.8) | collective-permute-done | bytes 800 | tf_op jit(solution)/shard_map/ppermute | solution.py:20
  289.8 1.9 collective-permute-start.9
  291.7 6.9 %collective-permute-done.9 = bf16[1248,2,32]{0,2,1:T(8,128)(2,1)S(1)} collective-permute-done((bf16[1248,2,32]{0,2,1:T(8,128)(2,1)S(1)}, bf16[1248,2,32]{0,2,1:T(8,128)(2,1)S(1)}, u32[]{:S(2)}, u32[]{:S(2)}) %collective-permute-start.9) | collective-permute-done | bytes 159776 | tf_op jit(solution)/shard_map/ppermute | solution.py:14
  300.0 2.0 collective-permute-done.10
  302.0 2.2 collective-permute-start.11
  308.3 3.5 reshape.73
  311.7 2.5 fusion.16
  314.3 3.4 collective-permute-start.12
  317.7 2.2 collective-permute-done.12
  319.9 4.1 collective-permute-start.13
  325.0 7.8 %collective-permute-done.14 = bf16[2,64,3,1]{1,3,2,0:T(2,128)(2,1)S(1)} collective-permute-done((bf16[2,64,3,1]{1,3,2,0:T(2,128)(2,1)S(1)}, bf16[2,64,3,1]{1,3,2,0:T(2,128)(2,1)S(1)}, u32[]{:S(2)}, u32[]{:S(2)}) %collective-permute-start.14) | collective-permute-done | bytes 800 | tf_op jit(solution)/shard_map/ppermute | solution.py:20
  335.1 2.7 multiply_bitcast_fusion
  337.8 7.9 %copy.64 = f32[64,2,78,2,4,2,4]{0,6,5,4,3,2,1:T(4,128)} copy(f32[64,2,78,2,4,2,4]{2,0,5,3,1,6,4:T(8,128)} %multiply_bitcast_fusion) | data formatting | bytes 5111808 | tf_op jit(solution)/shard_map/mul | solution.py:106
  345.7 271.5 %all-reduce.2.cloned.1.call-done = f32[64,9984]{0,1:T(8,128)} async-done(((f32[64,9984]{0,1:T(8,128)}), f32[64,9984]{0,1:T(8,128)}) %all-reduce.2.cloned.1.call-update) | async-done | bytes 2555920 | tf_op jit(solution)/shard_map/psum | solution.py:106
  617.2 4.7 constant_dynamic-slice_fusion
  621.9 3.9 copy.65
  (91 shorter events, 27.1 us)
Async XLA Ops:
  7.2 60.3 %all-gather.3.cloned.1.call-start = ((), (), s32[]{:S(2)}) async-start(), calls=%async_computation.1 | async-start | bytes 1357824 | tf_op jit(solution)/shard_map/all_gather | solution.py:52
  7.9 609.3 %all-reduce.2.cloned.1.call-start = ((), (), s32[]{:S(2)}) async-start(), calls=%async_computation | async-start | bytes 10223616 | tf_op jit(solution)/shard_map/psum | solution.py:106
  8.7 5.6 collective-permute-start
  14.3 2.1 collective-permute-start.1
  16.5 10.4 %collective-permute-start.2 = (bf16[2,64,3,1]{1,3,2,0:T(2,128)(2,1)S(1)}, bf16[2,64,3,1]{1,3,2,0:T(2,128)(2,1)S(1)}, u32[]{:S(2)}, u32[]{:S(2)}) collective-permute-start(bf16[2,64,3,1]{1,3,2,0:T(2,128)(2,1)S(1)} %pad_maximum_fusion.21), channel_id=1, source_target_pairs={{60,0},{0,4},{4,8},{8,12},{12,16},{16,20},{20,24},{24,28},{28,32},... | collective-permute-start | bytes 2312 | tf_op jit(solution)/shard_map/ppermute | solution.py:20
  245.6 10.2 %copy-start.1 = (f32[64]{0:T(128)S(1)}, f32[64]{0:T(128)}, u32[]{:S(2)}) copy-start(f32[64]{0:T(128)} %param.7) | copy-start | bytes 772
  247.3 7.2 %collective-permute-start.3 = (bf16[1248,2,32]{0,2,1:T(8,128)(2,1)S(1)}, bf16[1248,2,32]{0,2,1:T(8,128)(2,1)S(1)}, u32[]{:S(2)}, u32[]{:S(2)}) collective-permute-start(bf16[1248,2,32]{0,2,1:T(8,128)(2,1)S(1)} %bitcast.120), channel_id=1, source_target_pairs={{1,0},{2,1},{3,2},{5,4},{6,5},{7,6},{9,8},{10,9},{11,10},{13,12},{... | collective-permute-start | bytes 479240 | tf_op jit(solution)/shard_map/ppermute | solution.py:14
  254.6 3.3 collective-permute-start.4
  257.9 5.5 collective-permute-start.5
  265.5 3.5 copy-start
  270.9 5.6 collective-permute-start.6
  276.5 3.0 collective-permute-start.7
  279.5 8.2 %collective-permute-start.8 = (bf16[2,64,3,1]{1,3,2,0:T(2,128)(2,1)S(1)}, bf16[2,64,3,1]{1,3,2,0:T(2,128)(2,1)S(1)}, u32[]{:S(2)}, u32[]{:S(2)}) collective-permute-start(bf16[2,64,3,1]{1,3,2,0:T(2,128)(2,1)S(1)} %pad_maximum_fusion.20), channel_id=1, source_target_pairs={{60,0},{0,4},{4,8},{8,12},{12,16},{16,20},{20,24},{24,28},{28,32},... | collective-permute-start | bytes 2312 | tf_op jit(solution)/shard_map/ppermute | solution.py:20
  289.8 8.9 %collective-permute-start.9 = (bf16[1248,2,32]{0,2,1:T(8,128)(2,1)S(1)}, bf16[1248,2,32]{0,2,1:T(8,128)(2,1)S(1)}, u32[]{:S(2)}, u32[]{:S(2)}) collective-permute-start(bf16[1248,2,32]{0,2,1:T(8,128)(2,1)S(1)} %bitcast.127), channel_id=1, source_target_pairs={{1,0},{2,1},{3,2},{5,4},{6,5},{7,6},{9,8},{10,9},{11,10},{13,12},{... | collective-permute-start | bytes 479240 | tf_op jit(solution)/shard_map/ppermute | solution.py:14
  298.7 3.3 collective-permute-start.10
  302.0 4.2 collective-permute-start.11
  314.3 5.6 collective-permute-start.12
  319.9 5.0 collective-permute-start.13
  324.9 7.9 %collective-permute-start.14 = (bf16[2,64,3,1]{1,3,2,0:T(2,128)(2,1)S(1)}, bf16[2,64,3,1]{1,3,2,0:T(2,128)(2,1)S(1)}, u32[]{:S(2)}, u32[]{:S(2)}) collective-permute-start(bf16[2,64,3,1]{1,3,2,0:T(2,128)(2,1)S(1)} %pad_maximum_fusion.19), channel_id=1, source_target_pairs={{60,0},{0,4},{4,8},{8,12},{12,16},{16,20},{20,24},{24,28},{28,32},... | collective-permute-start | bytes 2312 | tf_op jit(solution)/shard_map/ppermute | solution.py:20
Sparse Core Ops, SparseCore 0:
  10.4 57.0 all-gather.2
  345.8 271.3 all-reduce.1
where the time goes:
time: 635 us; the launch traced here: 633 us
  waiting for transfers between devices  362 us (57%)
  local copies, waits for them, and re-layouts  210 us (33%)
  starting transfers between devices  32.7 us (5%)
  between operations  14.5 us (2%)
  matrix products  12.2 us (2%)
    psum x1, waiting for transfers between devices, body(): lax.psum(to_atoms(local, channels, atoms) * scale, ('lat', 'lon', 'tm'))  271 us
    reshape x1, local copies, waits for them, and re-layouts, body(): gathered.reshape(atoms, 2, channels, 2, 4, 2, 4)  89.3 us
    transpose x1, local copies, waits for them, and re-layouts, body(): blocks = gathered.reshape(atoms, 2, channels, 2, 4, 2, 4).transpose(1, 3,...  86.1 us
    all_gather x1, waiting for transfers between devices, body(): gathered = lax.all_gather(dictionary, 'lon', axis=0, tiled=True)  40.2 us
    ppermute x10, starting transfers between devices, passed_along(): return lax.ppermute(shard, axis, pairs)  24.8 us
    ppermute x10, waiting for transfers between devices, passed_along(): return lax.ppermute(shard, axis, pairs)  24.7 us
    ppermute x5, waiting for transfers between devices, shifted(): return lax.ppermute(block, axis, route)  24.7 us
  transfers between devices with their start and end apart: 17, of which 17 were waited for; matrix products, arithmetic and copies ran while one was open for 1% of the time, Pallas kernels for 0%

commit v1 on v0

--- a/solution.py
+++ b/solution.py
@@ -1,3 +1,4 @@
+import functools
 import math
 import jax
 import jax.numpy as jnp
@@ -6,6 +7,15 @@
 
 ITERS = 2
 STEP_SIZE = 0.5
+
+
+def wires_process(x_in, chip_axis, axis_name):
+    for num in (chip_axis, axis_name):
+        x_in = jax.lax.psum(x_in, num)
+    return x_in
+
+
+shifts_all_detail = functools.partial(wires_process, chip_axis=("lon", "tm"), axis_name="lat")
 
 
 def passed_along(shard, axis, by):
@@ -103,7 +113,7 @@
     local = lax.dot_general(
         residual, stacked, (((1,), (1,)), ((), ())), preferred_element_type=jnp.float32
     )
-    total = lax.psum(to_atoms(local, channels, atoms) * scale, ("lat", "lon", "tm"))
+    total = shifts_all_detail(to_atoms(local, channels, atoms) * scale)
     mine = lax.dynamic_slice_in_dim(total, lax.axis_index("lon") * owned_rows, owned_rows, 0)
     return (current.reshape(1, atoms, rows, columns), mine)
 

time: 635 us -> 1230 us (1.94)
  waiting for transfers between devices: 362 us -> 955 us
    psum x1 -> x2, waiting for transfers between devices: 271 us -> 864 us  [wires_process(): x_in = jax.lax.psum(x_in, num)]
  transfers between devices with their start and end apart: 17 -> 18, of which waited for: 17 -> 18; matrix products, arithmetic and copies ran while one was open for 1% -> 0% of each run, Pallas kernels for 0% -> 0%
where the time goes in v1:
time: 1230 us
  waiting for transfers between devices  955 us (78%)
  local copies, waits for them, and re-layouts  210 us (17%)
  starting transfers between devices  32.8 us (3%)
  between operations  14.2 us (1%)
    psum x2, waiting for transfers between devices, wires_process(): x_in = jax.lax.psum(x_in, num)  864 us
    reshape x1, local copies, waits for them, and re-layouts, body(): gathered.reshape(atoms, 2, channels, 2, 4, 2, 4)  89.3 us
    transpose x1, local copies, waits for them, and re-layouts, body(): blocks = gathered.reshape(atoms, 2, channels, 2, 4, 2, 4).transpose(1, 3,...  86.1 us
    all_gather x1, waiting for transfers between devices, body(): gathered = lax.all_gather(dictionary, 'lon', axis=0, tiled=True)  40.2 us
    ppermute x10, starting transfers between devices, passed_along(): return lax.ppermute(shard, axis, pairs)  24.8 us
    ppermute x10, waiting for transfers between devices, passed_along(): return lax.ppermute(shard, axis, pairs)  24.7 us
    ppermute x5, waiting for transfers between devices, shifted(): return lax.ppermute(block, axis, route)  24.7 us
  transfers between devices with their start and end apart: 18, of which 18 were waited for; matrix products, arithmetic and copies ran while one was open for 0% of the time, Pallas kernels for 0%

profile of v1, /device:TPU:2, one launch (start us, length us, event | category | flops | bytes accessed | tf_op | source)
XLA Modules:
  0.0 1225.1 jit_solution(17198893567389030809)
XLA Ops:
  8.7 3.4 collective-permute-start
  12.1 2.2 collective-permute-done
  21.6 5.3 collective-permute-done.2
  27.2 40.2 %all-gather.3.cloned.1.call-done = bf16[16,4,9984]{2,1,0:T(4,128)(2,1)} async-done(((bf16[1,4,9984]{2,1,0:T(4,128)(2,1)}), bf16[16,4,9984]{2,1,0:T(4,128)(2,1)}) %all-gather.3.cloned.1.call-update) | async-done | bytes 1277968 | tf_op jit(solution)/shard_map/all_gather | solution.py:62
  67.5 89.3 %reshape.84 = bf16[64,2,78,2,4,2,4]{6,5,4,3,2,1,0:T(2,128)(2,1)} reshape(bf16[16,4,9984]{2,1,0:T(4,128)(2,1)} %all-gather.3.cloned.1.call-done) | data formatting | bytes 2555904 | tf_op jit(solution)/shard_map/reshape | solution.py:65
  156.8 86.1 %copy.69 = bf16[64,2,78,2,4,2,4]{0,6,4,2,5,3,1:T(4,128)(2,1)S(1)} copy(bf16[64,2,78,2,4,2,4]{6,5,4,3,2,1,0:T(2,128)(2,1)} %reshape.84) | data formatting | bytes 2555904 | tf_op jit(solution)/shard_map/transpose | solution.py:66
  242.8 2.8 copy.51
  247.3 2.5 collective-permute-start.3
  249.8 4.7 collective-permute-done.3
  255.9 2.0 collective-permute-done.4
  257.9 3.9 collective-permute-start.5
  265.5 3.5 reshape.68
  270.9 3.4 collective-permute-start.6
  274.3 2.2 collective-permute-done.6
  276.5 2.2 collective-permute-start.7
  279.6 8.1 collective-permute-done.8
  289.8 1.9 collective-permute-start.9
  291.7 6.9 collective-permute-done.9
  300.0 2.0 collective-permute-done.10
  302.0 2.2 collective-permute-start.11
  308.3 3.5 reshape.73
  311.7 2.5 fusion.16
  314.3 3.4 collective-permute-start.12
  317.7 2.2 collective-permute-done.12
  319.9 4.1 collective-permute-start.13
  325.0 7.8 collective-permute-done.14
  335.1 2.7 multiply_bitcast_fusion
  337.8 7.9 copy.64
  345.8 754.3 %all-reduce.3.cloned.1.call-done = f32[64,9984]{0,1:T(8,128)} async-done(((f32[64,9984]{0,1:T(8,128)}), f32[64,9984]{0,1:T(8,128)}) %all-reduce.3.cloned.1.call-update) | async-done | bytes 2555920 | tf_op jit(solution)/shard_map/psum | solution.py:14
  1100.1 109.9 %all-reduce.5.cloned.1.call-done = f32[64,9984]{0,1:T(8,128)} async-done(((f32[64,9984]{0,1:T(8,128)}), f32[64,9984]{0,1:T(8,128)}) %all-reduce.5.cloned.1.call-update) | async-done | bytes 2555920 | tf_op jit(solution)/shard_map/psum | solution.py:14
  1210.0 4.7 constant_dynamic-slice_fusion
  1214.7 3.9 copy.65
  (94 shorter events, 29.1 us)
Async XLA Ops:
  7.2 60.3 %all-gather.3.cloned.1.call-start = ((), (), s32[]{:S(2)}) async-start(), calls=%async_computation.2 | async-start | bytes 1357824 | tf_op jit(solution)/shard_map/all_gather | solution.py:62
  7.9 1092.2 %all-reduce.3.cloned.1.call-start = ((), (), s32[]{:S(2)}) async-start(), calls=%async_computation | async-start | bytes 10223616 | tf_op jit(solution)/shard_map/psum | solution.py:14
  8.7 5.6 collective-permute-start
  14.3 2.1 collective-permute-start.1
  16.5 10.4 collective-permute-start.2
  245.6 10.2 copy-start.1
  247.3 7.2 collective-permute-start.3
  254.6 3.3 collective-permute-start.4
  257.9 5.5 collective-permute-start.5
  265.5 3.5 copy-start
  270.9 5.6 collective-permute-start.6
  276.5 3.0 collective-permute-start.7
  279.5 8.2 collective-permute-start.8
  289.8 8.9 collective-permute-start.9
  298.7 3.3 collective-permute-start.10
  302.0 4.2 collective-permute-start.11
  314.3 5.6 collective-permute-start.12
  319.9 5.0 collective-permute-start.13
  324.9 7.9 collective-permute-start.14
  345.7 864.3 %all-reduce.5.cloned.1.call-start = ((), (), s32[]{:S(2)}) async-start(), calls=%async_computation.1 | async-start | bytes 10223616 | tf_op jit(solution)/shard_map/psum | solution.py:14
Sparse Core Ops, SparseCore 0:
  10.4 57.0 all-gather.2
  345.8 754.1 all-reduce.2
  1102.8 107.2 all-reduce.4
